TPU v7x, 32 devices: a whole 2x2x4 slice. The times are simulated.
32 devices in a mesh: dp: 8 (over y, x, core), seq: 4 (over z).
Axes of the slice: x: 2, y: 2, z: 4, core: 2. Of those that a mesh axis runs over, the one named last changes fastest.
Arguments:
- inputs: bfloat16 [8, 1024, 768], P('dp', 'seq'), may hold values from -6 to 6
- d_out: bfloat16 [8, 1024, 768], P('dp', 'seq'), may hold values from -6 to 6
- segments: int32 [8, 1024], P('dp'), may hold values from 0 to 1023, as said below
- buckets: int32 [2048], replicated, may hold values from 0 to 31
- w_query: bfloat16 [768, 768], P(('dp', 'seq')), may hold values from -0.21875 to 0.21875
- w_key: bfloat16 [768, 768], P(('dp', 'seq')), may hold values from -0.21875 to 0.21875
- w_value: bfloat16 [768, 768], P(('dp', 'seq')), may hold values from -0.21875 to 0.21875
- w_out: bfloat16 [768, 768], P(('dp', 'seq')), may hold values from -1.75 to 1.75
- w_gate: bfloat16 [768, 2048], P(('dp', 'seq')), may hold values from -0.21875 to 0.21875
- w_up: bfloat16 [768, 2048], P(('dp', 'seq')), may hold values from -0.21875 to 0.21875
- w_down: bfloat16 [2048, 768], P(('dp', 'seq')), may hold values from -0.1875 to 0.1875
- gain_attn: float32 [768], replicated, may hold values from 0.1 to 1.9
- gain_ffn: float32 [768], replicated, may hold values from 0.1 to 1.9
- bias_table: float32 [32, 12], replicated, may hold values from -4 to 4
Outputs:
- output: bfloat16 [8, 1024, 768], P('dp', 'seq')
- d_inputs: float32 [8, 1024, 768], P('dp', 'seq')
- grad_query: float32 [768, 768], P(('dp', 'seq'))
- grad_key: float32 [768, 768], P(('dp', 'seq'))
- grad_value: float32 [768, 768], P(('dp', 'seq'))
- grad_out: float32 [768, 768], P(('dp', 'seq'))
- grad_gate: float32 [768, 2048], P(('dp', 'seq'))
- grad_up: float32 [768, 2048], P(('dp', 'seq'))
- grad_down: float32 [2048, 768], P(('dp', 'seq'))
- grad_gain_attn: float32 [768], replicated
- grad_gain_ffn: float32 [768], replicated
- grad_table: float32 [32, 12], replicated
Inputs may be any that keep to these rules, and one draw needn't show every extreme that they name: `segments`: each row's label is the index of the last row of its document within the sequence; labels never fall along a sequence, and rows share a document exactly when they share a label.
All inputs are finite; a program needn't handle non-finite values.
Results may differ from a plain program's by a relative error of at most 0.015.
Values may be sent and summed in bfloat16 or wider, within the bound.
No kernel may reach another device: no remote copies, remote signals or barrier semaphores. Data moves between devices by JAX's collectives and lax.ppermute only.
A program may use at most 192 MiB of HBM per device.

v0:
```python
import jax
import jax.numpy as jnp
from jax import lax
from jax.sharding import PartitionSpec as P

EPS = 1e-06
MASKED = -1000000000.0
HIGHEST = lax.Precision.HIGHEST


def norm_rows(values, gain):
    return values * lax.rsqrt(jnp.mean(values * values, axis=-1, keepdims=True) + EPS) * gain


def geglu(gate_act, up_act):
    return jax.nn.gelu(gate_act, approximate=True) * up_act


def matmul(left, right):
    return jnp.dot(left, right, preferred_element_type=jnp.float32)


def left_matmul(left, right):
    return lax.dot_general(
        left, right, (((0,), (0,)), ((), ())), preferred_element_type=jnp.float32
    )


def right_matmul(left, right):
    return lax.dot_general(
        left, right, (((1,), (1,)), ((), ())), preferred_element_type=jnp.float32
    )


def shifted_bias(per_dist, query_count, key_count):
    head_count, width = per_dist.shape
    flipped = per_dist[:, ::-1]
    tiled = jnp.tile(flipped, (1, query_count + 1))[:, : query_count * (width + 1)]
    rows = tiled.reshape(head_count, query_count, width + 1)[:, :, :key_count]
    return rows[:, :, ::-1]


def diagonal_sums(scores):
    head_count, row_count, col_count = scores.shape
    row_width = row_count + col_count
    padded = jnp.concatenate(
        [jnp.zeros((head_count, row_count, row_count), scores.dtype), scores], axis=2
    )
    flat_rows = jnp.concatenate(
        [
            padded.reshape(head_count, row_count * row_width),
            jnp.zeros((head_count, row_count), scores.dtype),
        ],
        axis=1,
    )
    skewed = flat_rows.reshape(head_count, row_count, row_width + 1)
    return jnp.sum(skewed, axis=1)[:, 1:row_width]


def block_parts(
    queries,
    key_heads,
    value_heads,
    seg_query,
    seg_all,
    buckets,
    table,
    first_row,
    blk_index,
    key_block,
):
    query_count = queries.shape[0]
    seq_len = key_heads.shape[0]
    scale = queries.shape[-1] ** (-0.5)
    key_start = blk_index * key_block
    key_blk = lax.dynamic_slice_in_dim(key_heads, key_start, key_block)
    value_blk = lax.dynamic_slice_in_dim(value_heads, key_start, key_block)
    seg_keys = lax.dynamic_slice_in_dim(seg_all, key_start, key_block)
    dist_base = key_start - first_row - query_count + 1 + seq_len
    window = lax.dynamic_slice_in_dim(buckets, dist_base, query_count + key_block - 1)
    onehot = (window[:, None] == jnp.arange(table.shape[0], dtype=jnp.int32)[None, :]).astype(
        jnp.float32
    )
    per_dist = jnp.dot(onehot, table, precision=HIGHEST).T
    bias_blk = shifted_bias(per_dist, query_count, key_block)
    raw_scores = (
        jnp.einsum("qhd,khd->hqk", queries, key_blk, preferred_element_type=jnp.float32) * scale
        + bias_blk
    )
    same_doc = (seg_query[:, None] == seg_keys[None, :])[None]
    weights_exp = jnp.exp(jnp.where(same_doc, raw_scores, MASKED))
    return (key_blk, value_blk, onehot, weights_exp)


def local(
    inputs,
    d_out,
    segments,
    buckets,
    w_query,
    w_key,
    w_value,
    w_out,
    w_gate,
    w_up,
    w_down,
    gain_attn,
    gain_ffn,
    bias_table,
):
    seq_count, row_count, model_width = inputs.shape
    seq_len = segments.shape[1]
    head_count = bias_table.shape[1]
    head_dim = model_width // head_count
    key_block = min(512, seq_len)
    block_count = seq_len // key_block
    token_count = seq_count * row_count
    scale = head_dim ** (-0.5)
    first_row = lax.axis_index("seq") * row_count
    blk_ids = jnp.arange(block_count, dtype=jnp.int32)
    gathered = (
        lax.all_gather(w_query, ("dp", "seq"), axis=0, tiled=True),
        lax.all_gather(w_key, ("dp", "seq"), axis=0, tiled=True),
        lax.all_gather(w_value, ("dp", "seq"), axis=0, tiled=True),
        lax.all_gather(w_out, ("dp", "seq"), axis=0, tiled=True),
        lax.all_gather(w_gate, ("dp", "seq"), axis=0, tiled=True),
        lax.all_gather(w_up, ("dp", "seq"), axis=0, tiled=True),
        lax.all_gather(w_down, ("dp", "seq"), axis=0, tiled=True),
    )
    full_query, full_key, full_value, full_out, full_gate, full_up, full_down = gathered
    flat_in = inputs.reshape(token_count, model_width).astype(jnp.float32)
    normed = norm_rows(flat_in, gain_attn).astype(jnp.bfloat16)
    queries = matmul(normed, full_query).astype(jnp.bfloat16)
    key_rows = (
        matmul(normed, full_key).astype(jnp.bfloat16).reshape(seq_count, row_count, model_width)
    )
    value_rows = (
        matmul(normed, full_value).astype(jnp.bfloat16).reshape(seq_count, row_count, model_width)
    )
    key_all, value_all = (
        lax.all_gather(key_rows, "seq", axis=1, tiled=True),
        lax.all_gather(value_rows, "seq", axis=1, tiled=True),
    )
    query_heads = queries.reshape(seq_count, row_count, head_count, head_dim)
    key_heads = key_all.reshape(seq_count, seq_len, head_count, head_dim)
    value_heads = value_all.reshape(seq_count, seq_len, head_count, head_dim)
    seg_queries = lax.dynamic_slice_in_dim(segments, first_row, row_count, axis=1)

    def attend(packed):
        query_one, key_one, value_one, seg_query, seg_all = packed

        def step(state_in, blk_index):
            totals, summed = state_in
            _, value_blk, _, weights_exp = block_parts(
                query_one,
                key_one,
                value_one,
                seg_query,
                seg_all,
                buckets,
                bias_table,
                first_row,
                blk_index,
                key_block,
            )
            summed = summed + jnp.einsum(
                "hqk,khd->qhd",
                weights_exp.astype(jnp.bfloat16),
                value_blk,
                preferred_element_type=jnp.float32,
            )
            totals = totals + jnp.sum(weights_exp, axis=-1)
            return ((totals, summed), None)

        start_state = (
            jnp.zeros((head_count, row_count), jnp.float32),
            jnp.zeros((row_count, head_count, head_dim), jnp.float32),
        )
        (totals, summed), _ = lax.scan(step, start_state, blk_ids)
        return (summed / jnp.transpose(totals)[:, :, None], totals)

    attn_f32, totals_all = lax.map(
        attend, (query_heads, key_heads, value_heads, seg_queries, segments)
    )
    attn_rows = attn_f32.reshape(token_count, model_width).astype(jnp.bfloat16)
    mixed_rows = flat_in + matmul(attn_rows, full_out)
    normed_two = norm_rows(mixed_rows, gain_ffn).astype(jnp.bfloat16)
    gate_act = matmul(normed_two, full_gate)
    up_act = matmul(normed_two, full_up)
    hidden = geglu(gate_act, up_act).astype(jnp.bfloat16)
    result = mixed_rows + matmul(hidden, full_down)
    output = result.astype(jnp.bfloat16).reshape(seq_count, row_count, model_width)
    back_weights = (
        lax.all_gather(w_query, ("dp", "seq"), axis=0, tiled=True),
        lax.all_gather(w_key, ("dp", "seq"), axis=0, tiled=True),
        lax.all_gather(w_value, ("dp", "seq"), axis=0, tiled=True),
        lax.all_gather(w_out, ("dp", "seq"), axis=0, tiled=True),
        lax.all_gather(w_gate, ("dp", "seq"), axis=0, tiled=True),
        lax.all_gather(w_up, ("dp", "seq"), axis=0, tiled=True),
        lax.all_gather(w_down, ("dp", "seq"), axis=0, tiled=True),
    )
    back_query, back_key, back_value, back_out, back_gate, back_up, back_down = back_weights
    d_res = d_out.reshape(token_count, model_width)
    grad_down = left_matmul(hidden, d_res)
    d_hidden = right_matmul(d_res, back_down)
    _, geglu_back = jax.vjp(geglu, gate_act, up_act)
    d_gate, d_up = geglu_back(d_hidden)
    d_gate = d_gate.astype(jnp.bfloat16)
    d_up = d_up.astype(jnp.bfloat16)
    grad_gate = left_matmul(normed_two, d_gate)
    grad_up = left_matmul(normed_two, d_up)
    d_normed_two = right_matmul(d_gate, back_gate) + right_matmul(d_up, back_up)
    _, norm_two_back = jax.vjp(norm_rows, mixed_rows, gain_ffn)
    d_mixed_norm, grad_gain_ffn = norm_two_back(d_normed_two)
    d_mixed = d_res.astype(jnp.float32) + d_mixed_norm
    d_branch = d_mixed.astype(jnp.bfloat16)
    grad_out = left_matmul(attn_rows, d_branch)
    d_attn = right_matmul(d_branch, back_out).reshape(seq_count, row_count, head_count, head_dim)
    totals_rows = jnp.transpose(totals_all, (0, 2, 1))
    d_unnorm_all = (d_attn / totals_rows[:, :, :, None]).astype(jnp.bfloat16)
    correction_all = -jnp.sum(d_attn * attn_f32, axis=-1) / totals_rows

    def attend_back(packed):
        query_one, key_one, value_one, seg_query, seg_all, d_unnorm, corr_rows = packed
        correction = jnp.transpose(corr_rows)

        def step(state_in, blk_index):
            d_query, d_table = state_in
            key_blk, value_blk, onehot, weights_exp = block_parts(
                query_one,
                key_one,
                value_one,
                seg_query,
                seg_all,
                buckets,
                bias_table,
                first_row,
                blk_index,
                key_block,
            )
            d_prob = jnp.einsum(
                "qhd,khd->hqk", d_unnorm, value_blk, preferred_element_type=jnp.float32
            )
            d_raw = (weights_exp * (d_prob + correction[:, :, None])).astype(jnp.bfloat16)
            d_query = (
                d_query
                + jnp.einsum("hqk,khd->qhd", d_raw, key_blk, preferred_element_type=jnp.float32)
                * scale
            )
            d_table = d_table + jnp.dot(
                diagonal_sums(d_raw.astype(jnp.float32)), onehot, precision=HIGHEST
            )
            d_key = (
                jnp.einsum("hqk,qhd->khd", d_raw, query_one, preferred_element_type=jnp.float32)
                * scale
            )
            d_value = jnp.einsum(
                "hqk,qhd->khd",
                weights_exp.astype(jnp.bfloat16),
                d_unnorm,
                preferred_element_type=jnp.float32,
            )
            return ((d_query, d_table), (d_key, d_value))

        start_state = (
            jnp.zeros((row_count, head_count, head_dim), jnp.float32),
            jnp.zeros((head_count, bias_table.shape[0]), jnp.float32),
        )
        (d_query, d_table), key_parts = lax.scan(step, start_state, blk_ids)
        d_key, d_value = key_parts
        return (
            d_query,
            d_table,
            d_key.reshape(seq_len, model_width),
            d_value.reshape(seq_len, model_width),
        )

    back_inputs = (
        query_heads,
        key_heads,
        value_heads,
        seg_queries,
        segments,
        d_unnorm_all,
        correction_all,
    )
    d_query_all, d_table_all, d_key_all, d_value_all = lax.map(attend_back, back_inputs)
    d_key_own, d_value_own = (
        lax.psum_scatter(
            d_key_all.astype(jnp.bfloat16), "seq", scatter_dimension=1, tiled=True
        ).astype(jnp.float32),
        lax.psum_scatter(
            d_value_all.astype(jnp.bfloat16), "seq", scatter_dimension=1, tiled=True
        ).astype(jnp.float32),
    )
    d_query_b = d_query_all.reshape(token_count, model_width).astype(jnp.bfloat16)
    d_key_b = d_key_own.reshape(token_count, model_width).astype(jnp.bfloat16)
    d_value_b = d_value_own.reshape(token_count, model_width).astype(jnp.bfloat16)
    grad_query = left_matmul(normed, d_query_b)
    grad_key = left_matmul(normed, d_key_b)
    grad_value = left_matmul(normed, d_value_b)
    d_normed = (
        right_matmul(d_query_b, back_query)
        + right_matmul(d_key_b, back_key)
        + right_matmul(d_value_b, back_value)
    )
    _, norm_one_back = jax.vjp(norm_rows, flat_in, gain_attn)
    d_in_norm, grad_gain_attn = norm_one_back(d_normed)
    d_inputs = (d_mixed + d_in_norm).reshape(seq_count, row_count, model_width)
    owned = (
        lax.psum_scatter(grad_query, ("dp", "seq"), scatter_dimension=0, tiled=True),
        lax.psum_scatter(grad_key, ("dp", "seq"), scatter_dimension=0, tiled=True),
        lax.psum_scatter(grad_value, ("dp", "seq"), scatter_dimension=0, tiled=True),
        lax.psum_scatter(grad_out, ("dp", "seq"), scatter_dimension=0, tiled=True),
        lax.psum_scatter(grad_gate, ("dp", "seq"), scatter_dimension=0, tiled=True),
        lax.psum_scatter(grad_up, ("dp", "seq"), scatter_dimension=0, tiled=True),
        lax.psum_scatter(grad_down, ("dp", "seq"), scatter_dimension=0, tiled=True),
    )
    table_local = jnp.transpose(jnp.sum(d_table_all, axis=0))
    gain_one, gain_two, table_grad = lax.psum(
        (grad_gain_attn, grad_gain_ffn, table_local), ("dp", "seq")
    )
    return (
        output,
        d_inputs,
        owned[0],
        owned[1],
        owned[2],
        owned[3],
        owned[4],
        owned[5],
        owned[6],
        gain_one,
        gain_two,
        table_grad,
    )


def solution(mesh):
    return jax.shard_map(
        local,
        mesh=mesh,
        in_specs=(
            P("dp", "seq", None),
            P("dp", "seq", None),
            P("dp", None),
            P(),
            P(("dp", "seq"), None),
            P(("dp", "seq"), None),
            P(("dp", "seq"), None),
            P(("dp", "seq"), None),
            P(("dp", "seq"), None),
            P(("dp", "seq"), None),
            P(("dp", "seq"), None),
            P(),
            P(),
            P(),
        ),
        out_specs=(
            P("dp", "seq", None),
            P("dp", "seq", None),
            P(("dp", "seq"), None),
            P(("dp", "seq"), None),
            P(("dp", "seq"), None),
            P(("dp", "seq"), None),
            P(("dp", "seq"), None),
            P(("dp", "seq"), None),
            P(("dp", "seq"), None),
            P(),
            P(),
            P(),
        ),
        check_vma=False,
    )
```

profile of v0, /device:TPU:0, one launch (start us, length us, event | category | flops | bytes accessed | tf_op | source)
XLA Modules:
  0.0 1757.2 jit_solution(12982344528251555989)
XLA Ops:
  10.7 57.0 %all-gather.16.cloned.1.call-done = bf16[768,768]{1,0:T(8,128)(2,1)} async-done(((bf16[24,768]{1,0:T(8,128)(2,1)}), bf16[768,768]{1,0:T(8,128)(2,1)}) %all-gather.16.cloned.1.call-update) | async-done | bytes 1179664 | tf_op jit(solution)/shard_map/all_gather | solution.py:124
  70.4 53.1 %all-gather.12.cloned.1.call-done = bf16[768,768]{1,0:T(8,128)(2,1)} async-done(((bf16[24,768]{1,0:T(8,128)(2,1)}), bf16[768,768]{1,0:T(8,128)(2,1)}) %all-gather.12.cloned.1.call-update) | async-done | bytes 1179664 | tf_op jit(solution)/shard_map/all_gather | solution.py:123
  130.3 49.1 %all-gather.14.cloned.1.call-done = bf16[768,768]{1,0:T(8,128)(2,1)} async-done(((bf16[24,768]{1,0:T(8,128)(2,1)}), bf16[768,768]{1,0:T(8,128)(2,1)}) %all-gather.14.cloned.1.call-update) | async-done | bytes 1179664 | tf_op jit(solution)/shard_map/all_gather | solution.py:122
  181.4 35.5 %all-gather.28.cloned.1.call-done = bf16[1024,768]{1,0:T(8,128)(2,1)} async-done(((bf16[256,768]{1,0:T(8,128)(2,1)}), bf16[1024,768]{1,0:T(8,128)(2,1)}) %all-gather.28.cloned.1.call-update) | async-done | bytes 1572880 | tf_op jit(solution)/shard_map/all_gather | solution.py:142
  218.6 36.3 %all-gather.26.cloned.1.call-done = bf16[1024,768]{1,0:T(8,128)(2,1)} async-done(((bf16[256,768]{1,0:T(8,128)(2,1)}), bf16[1024,768]{1,0:T(8,128)(2,1)}) %all-gather.26.cloned.1.call-update) | async-done | bytes 1572880 | tf_op jit(solution)/shard_map/all_gather | solution.py:141
  257.1 241.5 %while.60 = (s32[]{:T(128)}, f32[12,256]{1,0:T(8,128)S(1)}, f32[256,12,64]{0,2,1:T(8,128)}, s32[256]{0:T(256)}, s32[2]{0:T(128)}, /*index=5*/s32[1024]{0:T(1024)...) while((s32[]{:T(128)}, f32[12,256]{1,0:T(8,128)S(1)}, ...), condition=%wide.region_3.4_spmd.clone, body=%wide.region_1.3_spmd.clone.sunk | while | flops 414603776 | bytes 133137936 | solution.py:179
  273.0 14.2 tile.39
  322.9 48.3 %rev.42 = f32[12,256,512]{1,2,0:T(8,128)} reverse(f32[12,256,512]{1,2,0:T(8,128)} %copy.69), dimensions={2} | reverse | bytes 12582912 | tf_op jit(solution)/shard_map/while/body/eval_jaxpr/while/body/eval_jaxpr/rev | solution.py:40
  443.5 48.3 %rev.42 = f32[12,256,512]{1,2,0:T(8,128)} reverse(f32[12,256,512]{1,2,0:T(8,128)} %copy.69), dimensions={2} | reverse | bytes 12582912 | tf_op jit(solution)/shard_map/while/body/eval_jaxpr/while/body/eval_jaxpr/rev | solution.py:40
  528.6 368.2 %while.61 = (s32[]{:T(128)}, f32[256,12,64]{0,2,1:T(8,128)}, f32[12,32]{1,0:T(8,128)}, bf16[2,512,12,64]{1,3,2,0:T(8,128)(2,1)}, bf16[2,512,12,64]{1,3,2,0:T(8,1...) while((s32[]{:T(128)}, f32[256,12,64]{0,2,1:T(8,128)}, ...), condition=%wide.region_9.10_spmd.clone, body=%wide.region_7.9_spmd.clone.sunk | while | flops 1030591232 | bytes 274231168 | solution.py:269
  613.7 48.3 %rev.43 = f32[12,256,512]{1,2,0:T(8,128)} reverse(f32[12,256,512]{1,2,0:T(8,128)} %copy.71), dimensions={2} | reverse | bytes 12582912 | tf_op jit(solution)/shard_map/while/body/eval_jaxpr/while/body/eval_jaxpr/rev | solution.py:40
  689.4 20.8 %reshape.329 = f32[12,256,769]{2,1,0:T(8,128)} reshape(f32[12,196864]{1,0:T(8,128)} %pad_convert_fusion.2) | data formatting | bytes 18898944 | tf_op jit(solution)/shard_map/while/body/eval_jaxpr/while/body/eval_jaxpr/reshape | solution.py:56
  783.6 48.3 %rev.43 = f32[12,256,512]{1,2,0:T(8,128)} reverse(f32[12,256,512]{1,2,0:T(8,128)} %copy.71), dimensions={2} | reverse | bytes 12582912 | tf_op jit(solution)/shard_map/while/body/eval_jaxpr/while/body/eval_jaxpr/rev | solution.py:40
  859.5 20.8 %reshape.329 = f32[12,256,769]{2,1,0:T(8,128)} reshape(f32[12,196864]{1,0:T(8,128)} %pad_convert_fusion.2) | data formatting | bytes 18898944 | tf_op jit(solution)/shard_map/while/body/eval_jaxpr/while/body/eval_jaxpr/reshape | solution.py:56
  913.2 23.5 %reduce-scatter.12.cloned.1.call-done = bf16[1,256,768]{1,2,0:T(8,128)(2,1)} async-done(((bf16[1,1024,768]{1,2,0:T(8,128)(2,1)}), bf16[1,256,768]{1,2,0:T(8,128)(2,1)}) %reduce-scatter.12.cloned.1.call-update) | async-done | bytes 393232 | tf_op jit(solution)/shard_map/reduce_scatter | solution.py:292
  939.9 33.5 %reduce-scatter.10.cloned.1.call-done = bf16[1,256,768]{1,2,0:T(8,128)(2,1)} async-done(((bf16[1,1024,768]{1,2,0:T(8,128)(2,1)}), bf16[1,256,768]{1,2,0:T(8,128)(2,1)}) %reduce-scatter.10.cloned.1.call-update) | async-done | bytes 393232 | tf_op jit(solution)/shard_map/reduce_scatter | solution.py:289
  998.0 39.6 %all-reduce.2 = (f32[768]{0:T(1024)}, f32[768]{0:T(1024)}, f32[32,12]{0,1:T(8,128)}) all-reduce(f32[768]{0:T(1024)S(1)} %get-tuple-element.776, f32[768]{0:T(1024)S(1)} %copy-done.44, f32[32,12]{0,1:T(8,128)S(1)} %bitcast.253), channel_id=1, replica_groups=mesh['dp'=8,'seq'=4] {'dp','seq'}, use_global_device_ids=true, to_apply=%region_21.22 | all-reduce | flops 1920 | bytes 15360 | tf_op jit(solution)/shard_map/psum | solution.py:320
  1038.7 38.5 %reduce-scatter.20.cloned.1.call-done = f32[24,768]{1,0:T(8,128)} async-done(((f32[768,768]{1,0:T(8,128)}), f32[24,768]{1,0:T(8,128)}) %reduce-scatter.20.cloned.1.call-update) | async-done | bytes 73744 | tf_op jit(solution)/shard_map/reduce_scatter | solution.py:314
  1077.2 104.8 %reduce-scatter.14.cloned.1.call-done = f32[24,768]{1,0:T(8,128)} async-done(((f32[768,768]{1,0:T(8,128)}), f32[24,768]{1,0:T(8,128)}) %reduce-scatter.14.cloned.1.call-update) | async-done | bytes 73744 | tf_op jit(solution)/shard_map/reduce_scatter | solution.py:311
  1181.9 103.8 %reduce-scatter.18.cloned.1.call-done = f32[24,768]{1,0:T(8,128)} async-done(((f32[768,768]{1,0:T(8,128)}), f32[24,768]{1,0:T(8,128)}) %reduce-scatter.18.cloned.1.call-update) | async-done | bytes 73744 | tf_op jit(solution)/shard_map/reduce_scatter | solution.py:313
  1285.8 104.6 %reduce-scatter.16.cloned.1.call-done = f32[24,768]{1,0:T(8,128)} async-done(((f32[768,768]{1,0:T(8,128)}), f32[24,768]{1,0:T(8,128)}) %reduce-scatter.16.cloned.1.call-update) | async-done | bytes 73744 | tf_op jit(solution)/shard_map/reduce_scatter | solution.py:312
  1390.3 119.4 %reduce-scatter.26.cloned.1.call-done = f32[64,768]{1,0:T(8,128)} async-done(((f32[2048,768]{1,0:T(8,128)}), f32[64,768]{1,0:T(8,128)}) %reduce-scatter.26.cloned.1.call-update) | async-done | bytes 196624 | tf_op jit(solution)/shard_map/reduce_scatter | solution.py:317
  1509.7 120.6 %reduce-scatter.24.cloned.1.call-done = f32[24,2048]{1,0:T(8,128)} async-done(((f32[768,2048]{1,0:T(8,128)}), f32[24,2048]{1,0:T(8,128)}) %reduce-scatter.24.cloned.1.call-update) | async-done | bytes 196624 | tf_op jit(solution)/shard_map/reduce_scatter | solution.py:316
  1630.3 119.9 %reduce-scatter.22.cloned.1.call-done = f32[24,2048]{1,0:T(8,128)} async-done(((f32[768,2048]{1,0:T(8,128)}), f32[24,2048]{1,0:T(8,128)}) %reduce-scatter.22.cloned.1.call-update) | async-done | bytes 196624 | tf_op jit(solution)/shard_map/reduce_scatter | solution.py:315
  (308 shorter events, 422.5 us)
Async XLA Ops:
  7.2 116.4 %copy-start.8 = (bf16[1,256,768]{2,1,0:T(8,128)(2,1)S(1)}, bf16[1,256,768]{2,1,0:T(8,128)(2,1)}, u32[]{:S(2)}) copy-start(bf16[1,256,768]{2,1,0:T(8,128)(2,1)} %param.18) | copy-start | bytes 1179652
  7.2 116.3 %copy-start.36 = (f32[768]{0:T(1024)S(1)}, f32[768]{0:T(1024)}, u32[]{:S(2)}) copy-start(f32[768]{0:T(1024)} %param.29) | copy-start | bytes 9220
  7.2 60.5 %all-gather.16.cloned.1.call-start = ((), (), s32[]{:S(2)}) async-start(), calls=%async_computation.11 | async-start | bytes 1216512 | tf_op jit(solution)/shard_map/all_gather | solution.py:124
  7.9 115.6 %all-gather.12.cloned.1.call-start = ((), (), s32[]{:S(2)}) async-start(), calls=%async_computation.9 | async-start | bytes 1216512 | tf_op jit(solution)/shard_map/all_gather | solution.py:123
  8.7 170.7 %all-gather.14.cloned.1.call-start = ((), (), s32[]{:S(2)}) async-start(), calls=%async_computation.10 | async-start | bytes 1216512 | tf_op jit(solution)/shard_map/all_gather | solution.py:122
  9.4 207.5 %all-gather.28.cloned.1.call-start = ((), (), s32[]{:S(2)}) async-start(), calls=%async_computation.26 | async-start | bytes 1966080 | tf_op jit(solution)/shard_map/all_gather | solution.py:142
  10.6 115.5 %copy-start.49 = (f32[256]{0:T(256)}, f32[256]{0:T(256)S(1)}, u32[]{:S(2)}) copy-start(f32[256]{0:T(256)S(1)} %fusion.50) | copy-start | bytes 3076
  10.6 168.8 %copy-start.42 = (f32[256]{0:T(256)}, f32[256]{0:T(256)S(1)}, u32[]{:S(2)}) copy-start(f32[256]{0:T(256)S(1)} %fusion.74) | copy-start | bytes 3076
  70.4 184.5 %all-gather.26.cloned.1.call-start = ((), (), s32[]{:S(2)}) async-start(), calls=%async_computation.25 | async-start | bytes 1966080 | tf_op jit(solution)/shard_map/all_gather | solution.py:141
  126.1 374.4 %all-gather.18.cloned.1.call-start = ((), (), s32[]{:S(2)}) async-start(), calls=%async_computation.12 | async-start | bytes 1216512 | tf_op jit(solution)/shard_map/all_gather | solution.py:125
  126.7 378.0 %all-gather.22.cloned.1.call-start = ((), (), s32[]{:S(2)}) async-start(), calls=%async_computation.14 | async-start | bytes 3244032 | tf_op jit(solution)/shard_map/all_gather | solution.py:127
  127.4 381.6 %all-gather.20.cloned.1.call-start = ((), (), s32[]{:S(2)}) async-start(), calls=%async_computation.13 | async-start | bytes 3244032 | tf_op jit(solution)/shard_map/all_gather | solution.py:126
  128.2 385.2 %all-gather.24.cloned.1.call-start = ((), (), s32[]{:S(2)}) async-start(), calls=%async_computation.15 | async-start | bytes 3244032 | tf_op jit(solution)/shard_map/all_gather | solution.py:128
  128.9 807.9 %reduce-scatter.12.cloned.1.call-start = ((), (), s32[]{:S(2)}) async-start(), calls=%async_computation.17 | async-start | bytes 1966080 | tf_op jit(solution)/shard_map/reduce_scatter | solution.py:292
  547.7 114.4 %copy-start.2 = (bf16[1024,12,64]{0,2,1:T(8,128)(2,1)}, bf16[1024,12,64]{0,2,1:T(8,128)(2,1)S(1)}, u32[]{:S(2)}) copy-start(bf16[1024,12,64]{0,2,1:T(8,128)(2,1)S(1)} %get-tuple-element.1132) | copy-start | bytes 4718596 | tf_op jit(solution)/shard_map/while/body/eval_jaxpr/while
  717.5 114.4 %copy-start.2 = (bf16[1024,12,64]{0,2,1:T(8,128)(2,1)}, bf16[1024,12,64]{0,2,1:T(8,128)(2,1)S(1)}, u32[]{:S(2)}) copy-start(bf16[1024,12,64]{0,2,1:T(8,128)(2,1)S(1)} %get-tuple-element.1132) | copy-start | bytes 4718596 | tf_op jit(solution)/shard_map/while/body/eval_jaxpr/while
  902.3 71.1 %reduce-scatter.10.cloned.1.call-start = ((), (), s32[]{:S(2)}) async-start(), calls=%async_computation.16 | async-start | bytes 1966080 | tf_op jit(solution)/shard_map/reduce_scatter | solution.py:289
  907.8 169.4 %reduce-scatter.20.cloned.1.call-start = ((), (), s32[]{:S(2)}) async-start(), calls=%async_computation.21 | async-start | bytes 2433024 | tf_op jit(solution)/shard_map/reduce_scatter | solution.py:314
  909.8 272.1 %reduce-scatter.14.cloned.1.call-start = ((), (), s32[]{:S(2)}) async-start(), calls=%async_computation.18 | async-start | bytes 2433024 | tf_op jit(solution)/shard_map/reduce_scatter | solution.py:311
  913.2 372.6 %reduce-scatter.18.cloned.1.call-start = ((), (), s32[]{:S(2)}) async-start(), calls=%async_computation.20 | async-start | bytes 2433024 | tf_op jit(solution)/shard_map/reduce_scatter | solution.py:313
  939.8 450.5 %reduce-scatter.16.cloned.1.call-start = ((), (), s32[]{:S(2)}) async-start(), calls=%async_computation.19 | async-start | bytes 2433024 | tf_op jit(solution)/shard_map/reduce_scatter | solution.py:312
  976.4 533.4 %reduce-scatter.26.cloned.1.call-start = ((), (), s32[]{:S(2)}) async-start(), calls=%async_computation.24 | async-start | bytes 6488064 | tf_op jit(solution)/shard_map/reduce_scatter | solution.py:317
  980.2 650.1 %reduce-scatter.24.cloned.1.call-start = ((), (), s32[]{:S(2)}) async-start(), calls=%async_computation.23 | async-start | bytes 6488064 | tf_op jit(solution)/shard_map/reduce_scatter | solution.py:316
  985.2 765.0 %reduce-scatter.22.cloned.1.call-start = ((), (), s32[]{:S(2)}) async-start(), calls=%async_computation.22 | async-start | bytes 6488064 | tf_op jit(solution)/shard_map/reduce_scatter | solution.py:315
  (63 other events, 395.3 us)
Sparse Core Ops, SparseCore 0:
  10.8 56.7 all-gather.15
  70.5 53.0 all-gather.11
  126.3 53.0 all-gather.13
  180.8 36.0 all-gather.27
  218.9 35.9 all-gather.25
  257.5 52.9 all-gather.17
  313.4 57.9 all-gather.21
  374.3 57.8 all-gather.19
  435.1 57.8 all-gather.23
  902.4 34.2 reduce-scatter.11
  939.1 34.2 reduce-scatter.9
  979.1 98.0 reduce-scatter.19
  1083.9 98.0 reduce-scatter.13
  1187.6 98.0 reduce-scatter.17
  1292.3 97.9 reduce-scatter.15
  1396.4 113.3 reduce-scatter.25
  1516.7 113.5 reduce-scatter.23
  1636.4 113.7 reduce-scatter.21
where the time goes:
time: 1780 us; the launch traced here: 1760 us
  waiting for transfers between devices  1000 us (56%)
  local copies, waits for them, and re-layouts  529 us (30%)
  matrix products  102 us (6%)
  blocking collectives  39.6 us (2%)
  other arithmetic  35 us (2%)
  loops' own time  31.6 us (2%)
    rev x4, local copies, waits for them, and re-layouts, shifted_bias(): return rows[:, :, ::-1]  193 us
    reduce_scatter x1, waiting for transfers between devices, local(): lax.psum_scatter(grad_up, ('dp', 'seq'), scatter_dimension=0, tiled=True)  121 us
    reduce_scatter x1, waiting for transfers between devices, local(): lax.psum_scatter(grad_gate, ('dp', 'seq'), scatter_dimension=0, tiled=True)  120 us
    reduce_scatter x1, waiting for transfers between devices, local(): lax.psum_scatter(grad_down, ('dp', 'seq'), scatter_dimension=0, tiled=True)  119 us
    while x82, local copies, waits for them, and re-layouts  113 us
    reduce_scatter x1, waiting for transfers between devices, local(): lax.psum_scatter(grad_query, ('dp', 'seq'), scatter_dimension=0, tiled=True)  105 us
    reduce_scatter x1, waiting for transfers between devices, local(): lax.psum_scatter(grad_key, ('dp', 'seq'), scatter_dimension=0, tiled=True)  105 us
    reduce_scatter x1, waiting for transfers between devices, local(): lax.psum_scatter(grad_value, ('dp', 'seq'), scatter_dimension=0, tiled=True)  104 us
  transfers between devices with their start and end apart: 18, of which 14 were waited for; matrix products, arithmetic and copies ran while one was open for 17% of the time, Pallas kernels for 0%

commit v1 on v0

--- a/solution.py
+++ b/solution.py
@@ -2,10 +2,35 @@
 import jax.numpy as jnp
 from jax import lax
 from jax.sharding import PartitionSpec as P
+from jax.lax import axis_index, axis_size, ppermute
 
 EPS = 1e-06
 MASKED = -1000000000.0
 HIGHEST = lax.Precision.HIGHEST
+
+
+def _treat_cells(my_tile, k_dim):
+    z1 = list(my_tile.shape[1:])
+    z1[k_dim] *= my_tile.shape[0]
+    return jnp.moveaxis(my_tile, 0, k_dim).reshape(z1)
+
+
+def cut_view(xin, lane_axis, ndim_at):
+    chips = axis_size(lane_axis)
+    ledger = tuple(((ii, (ii + 1) % chips) for ii in range(chips)))
+    made = tuple(((k0, m) for m, k0 in ledger))
+    inter, reached = ([], [])
+    for hop_no in range(chips - 1):
+        if hop_no % 2 == 0:
+            inter.append(ppermute(inter[-1] if inter else xin, axis_name=lane_axis, perm=ledger))
+        else:
+            reached.append(
+                ppermute(reached[-1] if reached else xin, axis_name=lane_axis, perm=made)
+            )
+    all_rows = jnp.stack([*inter[::-1], xin, *reached])
+    n_now = axis_index(lane_axis) - len(inter)
+    all_rows = all_rows[(jnp.arange(chips) - n_now) % chips]
+    return _treat_cells(all_rows, ndim_at)
 
 
 def norm_rows(values, gain):
@@ -139,7 +164,7 @@
     )
     key_all, value_all = (
         lax.all_gather(key_rows, "seq", axis=1, tiled=True),
-        lax.all_gather(value_rows, "seq", axis=1, tiled=True),
+        cut_view(value_rows, lane_axis="seq", ndim_at=1),
     )
     query_heads = queries.reshape(seq_count, row_count, head_count, head_dim)
     key_heads = key_all.reshape(seq_count, seq_len, head_count, head_dim)

time: 1780 us -> 1730 us (0.972)
  waiting for transfers between devices: 1000 us -> 962 us
  loops' own time: 31.6 us -> 13.2 us
    all_gather x1 -> x0, waiting for transfers between devices: 35.5 us -> none  [local(): lax.all_gather(value_rows, 'seq', axis=1, tiled=True)]
    another operation x1, loops' own time: 29.9 us -> 11 us  [attend_back(): (d_query, d_table), key_parts = lax.scan(step, start_state, blk_ids)]
  transfers between devices with their start and end apart: 18 -> 20, of which waited for: 14 -> 14; matrix products, arithmetic and copies ran while one was open for 17% -> 18% of each run, Pallas kernels for 0% -> 0%
where the time goes in v1:
time: 1730 us; the launch traced here: 1700 us
  waiting for transfers between devices  962 us (56%)
  local copies, waits for them, and re-layouts  533 us (31%)
  matrix products  101 us (6%)
  blocking collectives  39.6 us (2%)
  other arithmetic  35.8 us (2%)
    rev x4, local copies, waits for them, and re-layouts, shifted_bias(): return rows[:, :, ::-1]  193 us
    reduce_scatter x1, waiting for transfers between devices, local(): lax.psum_scatter(grad_up, ('dp', 'seq'), scatter_dimension=0, tiled=True)  121 us
    reduce_scatter x1, waiting for transfers between devices, local(): lax.psum_scatter(grad_gate, ('dp', 'seq'), scatter_dimension=0, tiled=True)  120 us
    reduce_scatter x1, waiting for transfers between devices, local(): lax.psum_scatter(grad_down, ('dp', 'seq'), scatter_dimension=0, tiled=True)  119 us
    while x82, local copies, waits for them, and re-layouts  113 us
    reduce_scatter x1, waiting for transfers between devices, local(): lax.psum_scatter(grad_key, ('dp', 'seq'), scatter_dimension=0, tiled=True)  105 us
    reduce_scatter x1, waiting for transfers between devices, local(): lax.psum_scatter(grad_query, ('dp', 'seq'), scatter_dimension=0, tiled=True)  105 us
    reduce_scatter x1, waiting for transfers between devices, local(): lax.psum_scatter(grad_value, ('dp', 'seq'), scatter_dimension=0, tiled=True)  104 us
  transfers between devices with their start and end apart: 20, of which 14 were waited for; matrix products, arithmetic and copies ran while one was open for 18% of the time, Pallas kernels for 0%

profile of v1, /device:TPU:0, one launch (start us, length us, event | category | flops | bytes accessed | tf_op | source)
XLA Modules:
  0.0 1704.5 jit_solution(8295543324982151573)
XLA Ops:
  10.7 57.0 %all-gather.10.cloned.1.call-done = bf16[768,768]{1,0:T(8,128)(2,1)} async-done(((bf16[24,768]{1,0:T(8,128)(2,1)}), bf16[768,768]{1,0:T(8,128)(2,1)}) %all-gather.10.cloned.1.call-update) | async-done | bytes 1179664 | tf_op jit(solution)/shard_map/all_gather | solution.py:148
  73.1 50.5 %all-gather.14.cloned.1.call-done = bf16[768,768]{1,0:T(8,128)(2,1)} async-done(((bf16[24,768]{1,0:T(8,128)(2,1)}), bf16[768,768]{1,0:T(8,128)(2,1)}) %all-gather.14.cloned.1.call-update) | async-done | bytes 1179664 | tf_op jit(solution)/shard_map/all_gather | solution.py:149
  140.1 43.0 %all-gather.12.cloned.1.call-done = bf16[768,768]{1,0:T(8,128)(2,1)} async-done(((bf16[24,768]{1,0:T(8,128)(2,1)}), bf16[768,768]{1,0:T(8,128)(2,1)}) %all-gather.12.cloned.1.call-update) | async-done | bytes 1179664 | tf_op jit(solution)/shard_map/all_gather | solution.py:147
  191.0 30.1 %all-gather.24.cloned.1.call-done = bf16[1024,768]{1,0:T(8,128)(2,1)} async-done(((bf16[256,768]{1,0:T(8,128)(2,1)}), bf16[1024,768]{1,0:T(8,128)(2,1)}) %all-gather.24.cloned.1.call-update) | async-done | bytes 1572880 | tf_op jit(solution)/shard_map/all_gather | solution.py:166
  223.3 241.9 %while.60 = (s32[]{:T(128)}, f32[12,256]{1,0:T(8,128)S(1)}, f32[256,12,64]{0,2,1:T(8,128)}, s32[256]{0:T(256)}, s32[2]{0:T(128)}, /*index=5*/s32[1024]{0:T(1024)...) while((s32[]{:T(128)}, f32[12,256]{1,0:T(8,128)S(1)}, ...), condition=%wide.region_3.4_spmd.clone, body=%wide.region_1.3_spmd.clone.sunk | while | flops 414603776 | bytes 133137936 | solution.py:204
  289.4 48.3 %rev.42 = f32[12,256,512]{1,2,0:T(8,128)} reverse(f32[12,256,512]{1,2,0:T(8,128)} %copy.69), dimensions={2} | reverse | bytes 12582912 | tf_op jit(solution)/shard_map/while/body/eval_jaxpr/while/body/eval_jaxpr/rev | solution.py:65
  360.0 14.2 tile.39
  410.0 48.3 %rev.42 = f32[12,256,512]{1,2,0:T(8,128)} reverse(f32[12,256,512]{1,2,0:T(8,128)} %copy.69), dimensions={2} | reverse | bytes 12582912 | tf_op jit(solution)/shard_map/while/body/eval_jaxpr/while/body/eval_jaxpr/rev | solution.py:65
  495.3 349.3 %while.61 = (s32[]{:T(128)}, f32[256,12,64]{0,2,1:T(8,128)}, f32[12,32]{1,0:T(8,128)}, bf16[2,512,12,64]{1,3,2,0:T(8,128)(2,1)}, bf16[2,512,12,64]{1,3,2,0:T(8,1...) while((s32[]{:T(128)}, f32[256,12,64]{0,2,1:T(8,128)}, ...), condition=%wide.region_9.10_spmd.clone, body=%wide.region_7.9_spmd.clone.sunk | while | flops 1030591232 | bytes 274231168 | solution.py:294
  511.7 14.2 tile.41
  561.6 48.3 %rev.43 = f32[12,256,512]{1,2,0:T(8,128)} reverse(f32[12,256,512]{1,2,0:T(8,128)} %copy.71), dimensions={2} | reverse | bytes 12582912 | tf_op jit(solution)/shard_map/while/body/eval_jaxpr/while/body/eval_jaxpr/rev | solution.py:65
  637.3 20.8 %reshape.386 = f32[12,256,769]{2,1,0:T(8,128)} reshape(f32[12,196864]{1,0:T(8,128)} %pad_convert_fusion.2) | data formatting | bytes 18898944 | tf_op jit(solution)/shard_map/while/body/eval_jaxpr/while/body/eval_jaxpr/reshape | solution.py:81
  731.4 48.3 %rev.43 = f32[12,256,512]{1,2,0:T(8,128)} reverse(f32[12,256,512]{1,2,0:T(8,128)} %copy.71), dimensions={2} | reverse | bytes 12582912 | tf_op jit(solution)/shard_map/while/body/eval_jaxpr/while/body/eval_jaxpr/rev | solution.py:65
  807.4 20.8 %reshape.386 = f32[12,256,769]{2,1,0:T(8,128)} reshape(f32[12,196864]{1,0:T(8,128)} %pad_convert_fusion.2) | data formatting | bytes 18898944 | tf_op jit(solution)/shard_map/while/body/eval_jaxpr/while/body/eval_jaxpr/reshape | solution.py:81
  861.1 23.5 %reduce-scatter.12.cloned.1.call-done = bf16[1,256,768]{1,2,0:T(8,128)(2,1)} async-done(((bf16[1,1024,768]{1,2,0:T(8,128)(2,1)}), bf16[1,256,768]{1,2,0:T(8,128)(2,1)}) %reduce-scatter.12.cloned.1.call-update) | async-done | bytes 393232 | tf_op jit(solution)/shard_map/reduce_scatter | solution.py:317
  887.7 33.3 %reduce-scatter.10.cloned.1.call-done = bf16[1,256,768]{1,2,0:T(8,128)(2,1)} async-done(((bf16[1,1024,768]{1,2,0:T(8,128)(2,1)}), bf16[1,256,768]{1,2,0:T(8,128)(2,1)}) %reduce-scatter.10.cloned.1.call-update) | async-done | bytes 393232 | tf_op jit(solution)/shard_map/reduce_scatter | solution.py:314
  945.7 39.6 %all-reduce.2 = (f32[768]{0:T(1024)}, f32[768]{0:T(1024)}, f32[32,12]{0,1:T(8,128)}) all-reduce(f32[768]{0:T(1024)S(1)} %get-tuple-element.776, f32[768]{0:T(1024)S(1)} %copy-done.44, f32[32,12]{0,1:T(8,128)S(1)} %bitcast.268), channel_id=1, replica_groups=mesh['dp'=8,'seq'=4] {'dp','seq'}, use_global_device_ids=true, to_apply=%region_21.22 | all-reduce | flops 1920 | bytes 15360 | tf_op jit(solution)/shard_map/psum | solution.py:345
  986.4 38.5 %reduce-scatter.20.cloned.1.call-done = f32[24,768]{1,0:T(8,128)} async-done(((f32[768,768]{1,0:T(8,128)}), f32[24,768]{1,0:T(8,128)}) %reduce-scatter.20.cloned.1.call-update) | async-done | bytes 73744 | tf_op jit(solution)/shard_map/reduce_scatter | solution.py:339
  1024.9 104.7 %reduce-scatter.14.cloned.1.call-done = f32[24,768]{1,0:T(8,128)} async-done(((f32[768,768]{1,0:T(8,128)}), f32[24,768]{1,0:T(8,128)}) %reduce-scatter.14.cloned.1.call-update) | async-done | bytes 73744 | tf_op jit(solution)/shard_map/reduce_scatter | solution.py:336
  1129.6 103.9 %reduce-scatter.18.cloned.1.call-done = f32[24,768]{1,0:T(8,128)} async-done(((f32[768,768]{1,0:T(8,128)}), f32[24,768]{1,0:T(8,128)}) %reduce-scatter.18.cloned.1.call-update) | async-done | bytes 73744 | tf_op jit(solution)/shard_map/reduce_scatter | solution.py:338
  1233.5 104.7 %reduce-scatter.16.cloned.1.call-done = f32[24,768]{1,0:T(8,128)} async-done(((f32[768,768]{1,0:T(8,128)}), f32[24,768]{1,0:T(8,128)}) %reduce-scatter.16.cloned.1.call-update) | async-done | bytes 73744 | tf_op jit(solution)/shard_map/reduce_scatter | solution.py:337
  1338.2 119.4 %reduce-scatter.26.cloned.1.call-done = f32[64,768]{1,0:T(8,128)} async-done(((f32[2048,768]{1,0:T(8,128)}), f32[64,768]{1,0:T(8,128)}) %reduce-scatter.26.cloned.1.call-update) | async-done | bytes 196624 | tf_op jit(solution)/shard_map/reduce_scatter | solution.py:342
  1457.6 120.5 %reduce-scatter.24.cloned.1.call-done = f32[24,2048]{1,0:T(8,128)} async-done(((f32[768,2048]{1,0:T(8,128)}), f32[24,2048]{1,0:T(8,128)}) %reduce-scatter.24.cloned.1.call-update) | async-done | bytes 196624 | tf_op jit(solution)/shard_map/reduce_scatter | solution.py:341
  1578.1 119.7 %reduce-scatter.22.cloned.1.call-done = f32[24,2048]{1,0:T(8,128)} async-done(((f32[768,2048]{1,0:T(8,128)}), f32[24,2048]{1,0:T(8,128)}) %reduce-scatter.22.cloned.1.call-update) | async-done | bytes 196624 | tf_op jit(solution)/shard_map/reduce_scatter | solution.py:340
  (316 shorter events, 425.0 us)
Async XLA Ops:
  7.2 116.4 %copy-start.8 = (bf16[1,256,768]{2,1,0:T(8,128)(2,1)S(1)}, bf16[1,256,768]{2,1,0:T(8,128)(2,1)}, u32[]{:S(2)}) copy-start(bf16[1,256,768]{2,1,0:T(8,128)(2,1)} %param.18) | copy-start | bytes 1179652
  7.2 116.3 %copy-start.36 = (f32[768]{0:T(1024)S(1)}, f32[768]{0:T(1024)}, u32[]{:S(2)}) copy-start(f32[768]{0:T(1024)} %param.29) | copy-start | bytes 9220
  7.2 60.5 %all-gather.10.cloned.1.call-start = ((), (), s32[]{:S(2)}) async-start(), calls=%async_computation.9 | async-start | bytes 1216512 | tf_op jit(solution)/shard_map/all_gather | solution.py:148
  7.9 115.6 %all-gather.14.cloned.1.call-start = ((), (), s32[]{:S(2)}) async-start(), calls=%async_computation.11 | async-start | bytes 1216512 | tf_op jit(solution)/shard_map/all_gather | solution.py:149
  8.7 174.3 %all-gather.12.cloned.1.call-start = ((), (), s32[]{:S(2)}) async-start(), calls=%async_computation.10 | async-start | bytes 1216512 | tf_op jit(solution)/shard_map/all_gather | solution.py:147
  9.4 211.7 %all-gather.24.cloned.1.call-start = ((), (), s32[]{:S(2)}) async-start(), calls=%async_computation.25 | async-start | bytes 1966080 | tf_op jit(solution)/shard_map/all_gather | solution.py:166
  10.6 114.7 %copy-start.49 = (f32[256]{0:T(256)}, f32[256]{0:T(256)S(1)}, u32[]{:S(2)}) copy-start(f32[256]{0:T(256)S(1)} %fusion.50) | copy-start | bytes 3076
  10.6 172.4 %copy-start.42 = (f32[256]{0:T(256)}, f32[256]{0:T(256)S(1)}, u32[]{:S(2)}) copy-start(f32[256]{0:T(256)S(1)} %fusion.74) | copy-start | bytes 3076
  70.4 396.9 %all-gather.16.cloned.1.call-start = ((), (), s32[]{:S(2)}) async-start(), calls=%async_computation.12 | async-start | bytes 1216512 | tf_op jit(solution)/shard_map/all_gather | solution.py:150
  71.0 400.4 %all-gather.20.cloned.1.call-start = ((), (), s32[]{:S(2)}) async-start(), calls=%async_computation.14 | async-start | bytes 3244032 | tf_op jit(solution)/shard_map/all_gather | solution.py:152
  71.5 404.2 %all-gather.18.cloned.1.call-start = ((), (), s32[]{:S(2)}) async-start(), calls=%async_computation.13 | async-start | bytes 3244032 | tf_op jit(solution)/shard_map/all_gather | solution.py:151
  72.3 407.8 %all-gather.22.cloned.1.call-start = ((), (), s32[]{:S(2)}) async-start(), calls=%async_computation.15 | async-start | bytes 3244032 | tf_op jit(solution)/shard_map/all_gather | solution.py:153
  73.0 811.6 %reduce-scatter.12.cloned.1.call-start = ((), (), s32[]{:S(2)}) async-start(), calls=%async_computation.17 | async-start | bytes 1966080 | tf_op jit(solution)/shard_map/reduce_scatter | solution.py:317
  125.3 14.1 collective-permute-start
  127.2 57.8 %collective-permute-start.2 = (bf16[1,256,768]{2,1,0:T(8,128)(2,1)S(1)}, bf16[1,256,768]{2,1,0:T(8,128)(2,1)S(1)}, u32[]{:S(2)}, u32[]{:S(2)}) collective-permute-start(bf16[1,256,768]{2,1,0:T(8,128)(2,1)S(1)} %bitcast.261), channel_id=1, source_target_pairs={{1,0},{2,1},{3,2},{0,3},{5,4},{6,5},{7,6},{4,7},{9,8},{10,9},{11,1... | collective-permute-start | bytes 1179656 | tf_op jit(solution)/shard_map/ppermute | solution.py:28
  139.4 45.6 %collective-permute-start.1 = (bf16[1,256,768]{2,1,0:T(8,128)(2,1)S(1)}, bf16[1,256,768]{2,1,0:T(8,128)(2,1)S(1)}, u32[]{:S(2)}, u32[]{:S(2)}) collective-permute-start(bf16[1,256,768]{2,1,0:T(8,128)(2,1)S(1)} %collective-permute-done), channel_id=1, source_target_pairs={{0,1},{1,2},{2,3},{3,0},{4,5},{5,6},{6,7},{7,4},{8,9},{9,10},{10,1... | collective-permute-start | bytes 1179656 | tf_op jit(solution)/shard_map/ppermute | solution.py:25
  850.1 70.9 %reduce-scatter.10.cloned.1.call-start = ((), (), s32[]{:S(2)}) async-start(), calls=%async_computation.16 | async-start | bytes 1966080 | tf_op jit(solution)/shard_map/reduce_scatter | solution.py:314
  855.6 169.3 %reduce-scatter.20.cloned.1.call-start = ((), (), s32[]{:S(2)}) async-start(), calls=%async_computation.21 | async-start | bytes 2433024 | tf_op jit(solution)/shard_map/reduce_scatter | solution.py:339
  857.6 272.0 %reduce-scatter.14.cloned.1.call-start = ((), (), s32[]{:S(2)}) async-start(), calls=%async_computation.18 | async-start | bytes 2433024 | tf_op jit(solution)/shard_map/reduce_scatter | solution.py:336
  861.0 372.5 %reduce-scatter.18.cloned.1.call-start = ((), (), s32[]{:S(2)}) async-start(), calls=%async_computation.20 | async-start | bytes 2433024 | tf_op jit(solution)/shard_map/reduce_scatter | solution.py:338
  887.7 450.6 %reduce-scatter.16.cloned.1.call-start = ((), (), s32[]{:S(2)}) async-start(), calls=%async_computation.19 | async-start | bytes 2433024 | tf_op jit(solution)/shard_map/reduce_scatter | solution.py:337
  924.0 533.6 %reduce-scatter.26.cloned.1.call-start = ((), (), s32[]{:S(2)}) async-start(), calls=%async_computation.24 | async-start | bytes 6488064 | tf_op jit(solution)/shard_map/reduce_scatter | solution.py:342
  927.8 650.3 %reduce-scatter.24.cloned.1.call-start = ((), (), s32[]{:S(2)}) async-start(), calls=%async_computation.23 | async-start | bytes 6488064 | tf_op jit(solution)/shard_map/reduce_scatter | solution.py:341
  932.9 764.9 %reduce-scatter.22.cloned.1.call-start = ((), (), s32[]{:S(2)}) async-start(), calls=%async_computation.22 | async-start | bytes 6488064 | tf_op jit(solution)/shard_map/reduce_scatter | solution.py:340
  (65 other events, 623.9 us)
Sparse Core Ops, SparseCore 0:
  10.8 56.7 all-gather.9
  70.5 53.0 all-gather.13
  126.3 56.6 all-gather.11
  185.0 36.0 all-gather.23
  223.7 52.9 all-gather.15
  279.5 57.9 all-gather.19
  340.4 57.8 all-gather.17
  401.2 57.8 all-gather.21
  850.2 34.2 reduce-scatter.11
  886.7 34.2 reduce-scatter.9
  926.9 97.9 reduce-scatter.19
  1031.5 98.0 reduce-scatter.13
  1135.5 97.9 reduce-scatter.17
  1240.0 98.1 reduce-scatter.15
  1344.3 113.3 reduce-scatter.25
  1464.6 113.4 reduce-scatter.23
  1584.2 113.5 reduce-scatter.21
